TPU v7x, 32 devices: a whole 2x2x4 slice. The times are simulated.
32 devices in a mesh: pipe: 4 (over z), dp: 8 (over y, x, core).
Axes of the slice: x: 2, y: 2, z: 4, core: 2. Of those that a mesh axis runs over, the one named last changes fastest.
Arguments:
- saved: bfloat16 [2, 4, 1024, 4096], P(None, 'pipe', 'dp'), may hold values from -6 to 6
- grad_out: bfloat16 [1024, 4096], P('dp'), may hold values from -6 to 6
- gain: float32 [2, 4, 4096], P(None, 'pipe'), may hold values from 0.5 to 1.5
- w_value: bfloat16 [4, 4096, 512], P('pipe', 'dp'), may hold values from -0.09375 to 0.09375
Outputs:
- grad_x: bfloat16 [2, 4, 1024, 4096], P(None, 'pipe', 'dp')
- grad_w: float32 [4, 4096, 512], P('pipe', 'dp')
All inputs are finite; a program needn't handle non-finite values.
Results may differ from a plain program's by a relative error of at most 0.012.
Values may be sent and summed in bfloat16 or wider, within the bound.
A program may use at most 64 MiB of HBM per device.

v0:
```python
import jax
import jax.numpy as jnp
from jax import lax
from jax.sharding import PartitionSpec as P

HEAD = 128


def passed_along(value, axis, steps):
    count = lax.axis_size(axis)
    pairs = [(source, (source + steps) % count) for source in range(count)]
    return lax.ppermute(value, axis, pairs)


def normalize(x_rows, scale_row):
    x32 = x_rows.astype(jnp.float32)
    rinv = lax.rsqrt(jnp.mean(x32 * x32, axis=-1, keepdims=True) + 1e-05)
    normed = x32 * rinv
    return (rinv, normed, (normed * scale_row).astype(jnp.bfloat16))


def on_device(saved, grad_out, gain, w_value):
    npipe = lax.axis_size("pipe")
    section = lax.axis_index("pipe")
    w_full = lax.all_gather(w_value, "dp", axis=1, tiled=True)
    w_mat = w_full[0]
    tok = saved.shape[2]
    width = saved.shape[3]
    kv_width = w_mat.shape[1]
    blocks = 2
    rows = tok // blocks
    kv_heads = kv_width // HEAD
    group = width // kv_width

    def one_step(k, carry):
        incoming, grad_buf, dv_buf = carry
        second = k - (npipe - 1) + section
        first = second - npipe
        in_second = (second >= 0) & (second < blocks)
        in_first = (first >= 0) & (first < blocks)
        valid = in_second | in_first
        loop_id = jnp.where(in_second, 1, 0).astype(jnp.int32)
        block = jnp.clip(jnp.where(in_second, second, first), 0, blocks - 1)
        start = block * rows
        zero = jnp.zeros((), jnp.int32)
        x_rows = lax.dynamic_slice(
            saved, (loop_id, zero, start, zero), (1, 1, rows, width)
        ).reshape(rows, width)
        fresh = lax.dynamic_slice_in_dim(grad_out, start, rows, 0)
        dy = jnp.where(in_second & (section == npipe - 1), fresh, incoming)
        dy = jnp.where(valid, dy, jnp.zeros_like(dy))
        scale_row = lax.dynamic_index_in_dim(gain[:, 0], loop_id, 0, keepdims=False)
        rinv, normed, _ = normalize(x_rows, scale_row)
        dv = dy.astype(jnp.float32).reshape(rows, kv_heads, group, HEAD).sum(2)
        dv = dv.reshape(rows, kv_width).astype(jnp.bfloat16)
        dh = lax.dot_general(
            dv, w_mat, (((1,), (1,)), ((), ())), preferred_element_type=jnp.float32
        )
        dhg = dh * scale_row
        dx = dy.astype(jnp.float32) + rinv * (
            dhg - normed * jnp.mean(dhg * normed, axis=-1, keepdims=True)
        )
        dx = dx.astype(jnp.bfloat16)
        old_x = lax.dynamic_slice(grad_buf, (loop_id, start, zero), (1, rows, width))
        grad_buf = lax.dynamic_update_slice(
            grad_buf, jnp.where(valid, dx[None], old_x), (loop_id, start, zero)
        )
        old_v = lax.dynamic_slice(dv_buf, (loop_id, start, zero), (1, rows, kv_width))
        dv_buf = lax.dynamic_update_slice(
            dv_buf, jnp.where(valid, dv[None], old_v), (loop_id, start, zero)
        )
        outgoing = passed_along(dx, "pipe", -1)
        return (outgoing, grad_buf, dv_buf)

    carry = (
        jnp.zeros((rows, width), jnp.bfloat16),
        jnp.zeros((2, tok, width), jnp.bfloat16),
        jnp.zeros((2, tok, kv_width), jnp.bfloat16),
    )
    carry = lax.fori_loop(0, blocks + 2 * npipe - 1, one_step, carry)
    _, _, hidden = normalize(saved[:, 0], gain[:, 0][:, None, :])
    hidden = hidden.reshape(2 * tok, width)
    dv_all = carry[2].reshape(2 * tok, kv_width)
    full_grad = lax.dot_general(
        hidden, dv_all, (((0,), (0,)), ((), ())), preferred_element_type=jnp.float32
    )
    grad_w = lax.psum_scatter(full_grad[None], "dp", scatter_dimension=1, tiled=True)
    grad_x = carry[1][:, None]
    return (grad_x, grad_w)


def solution(mesh):
    return jax.shard_map(
        on_device,
        mesh=mesh,
        in_specs=(
            P(None, "pipe", "dp", None),
            P("dp", None),
            P(None, "pipe", None),
            P("pipe", "dp", None),
        ),
        out_specs=(P(None, "pipe", "dp", None), P("pipe", "dp", None)),
        check_vma=False,
    )
```

profile of v0, /device:TPU:0, one launch (start us, length us, event | category | flops | bytes accessed | tf_op | source)
XLA Modules:
  0.0 335.0 jit_solution(14461938813727482571)
XLA Ops:
  7.9 1.4 copy.19
  9.3 2.2 fusion.10
  11.6 37.6 %all-gather.2.cloned.1.call-done = bf16[1,4096,512]{2,1,0:T(8,128)(2,1)} async-done(((bf16[1,512,512]{2,1,0:T(8,128)(2,1)}), bf16[1,4096,512]{2,1,0:T(8,128)(2,1)}) %all-gather.2.cloned.1.call-update) | async-done | bytes 4194320 | tf_op jit(solution)/shard_map/all_gather | solution.py:25
  49.2 0.8 broadcast.66
  50.1 1.6 broadcast_in_dim.33
  51.6 198.6 %while.19 = (s32[]{:T(128)}, bf16[64,4096]{1,0:T(8,128)(2,1)}, bf16[2,128,4096]{2,1,0:T(8,128)(2,1)}, bf16[2,128,512]{2,1,0:T(8,128)(2,1)S(1)}, s32[]{:T(128)}, ...) while((s32[]{:T(128)}, bf16[64,4096]{1,0:T(8,128)(2,1)}, ...), condition=%wide.region_4.5_spmd, body=%wide.region_0.4_spmd.sunk | while | flops 274464864 | bytes 24761596 | solution.py:80
  51.8 0.7 constant_dynamic-slice_fusion.2
  52.6 1.3 convert_bitcast_fusion.2
  54.0 3.8 %fusion.26 = (f32[64]{0:T(128)S(1)}, f32[64,4096]{1,0:T(8,128)S(1)}) fusion(f32[64]{0:T(128)S(1)} %add_rsqrt_fusion.3, bf16[2,1,128,4096]{3,2,1,0:T(8,128)(2,1)S(1)} %get-tuple-element.368, s32[]{:T(128)S(6)} %select_n.181, s32[]{:T(128)S(6)} %select_n.183, f32[4096]{0:T(1024)S(1)} %bitcast.64, bf16[4096,512]{1,0:T(8,128)(2,1)} %get-tuple-element.369, ...), kind=kOutput, calls=%fused_computation.7.clone.1 | convolution fusion | flops 269746112 | bytes 5849608 | tf_op jit(solution)/shard_map/while/body/eval_jaxpr/dot_general | solution.py:56
  57.9 2.3 fusion.27
  60.2 3.2 collective-permute-start
  63.4 11.5 %collective-permute-done = bf16[64,4096]{1,0:T(8,128)(2,1)S(1)} collective-permute-done((bf16[64,4096]{1,0:T(8,128)(2,1)S(1)}, bf16[64,4096]{1,0:T(8,128)(2,1)S(1)}, u32[]{:S(2)}, u32[]{:S(2)}) %collective-permute-start) | collective-permute-done | bytes 524320 | tf_op jit(solution)/shard_map/while/body/eval_jaxpr/ppermute | solution.py:12
  75.0 0.8 copy-done.2
  76.0 0.7 constant_dynamic-slice_fusion.2
  76.7 1.3 convert_bitcast_fusion.2
  78.2 3.8 %fusion.26 = (f32[64]{0:T(128)S(1)}, f32[64,4096]{1,0:T(8,128)S(1)}) fusion(f32[64]{0:T(128)S(1)} %add_rsqrt_fusion.3, bf16[2,1,128,4096]{3,2,1,0:T(8,128)(2,1)S(1)} %get-tuple-element.368, s32[]{:T(128)S(6)} %select_n.181, s32[]{:T(128)S(6)} %select_n.183, f32[4096]{0:T(1024)S(1)} %bitcast.64, bf16[4096,512]{1,0:T(8,128)(2,1)} %get-tuple-element.369, ...), kind=kOutput, calls=%fused_computation.7.clone.1 | convolution fusion | flops 269746112 | bytes 5849608 | tf_op jit(solution)/shard_map/while/body/eval_jaxpr/dot_general | solution.py:56
  82.0 2.3 fusion.27
  84.4 4.1 %collective-permute-start = (bf16[64,4096]{1,0:T(8,128)(2,1)S(1)}, bf16[64,4096]{1,0:T(8,128)(2,1)S(1)}, u32[]{:S(2)}, u32[]{:S(2)}) collective-permute-start(bf16[64,4096]{1,0:T(8,128)(2,1)S(1)} %get-tuple-element.323), channel_id=1, source_target_pairs={{0,24},{8,0},{16,8},{24,16},{1,25},{9,1},{17,9},{25,17},{2,26},{10... | collective-permute-start | bytes 1572872 | tf_op jit(solution)/shard_map/while/body/eval_jaxpr/ppermute | solution.py:12
  88.6 10.7 %collective-permute-done = bf16[64,4096]{1,0:T(8,128)(2,1)S(1)} collective-permute-done((bf16[64,4096]{1,0:T(8,128)(2,1)S(1)}, bf16[64,4096]{1,0:T(8,128)(2,1)S(1)}, u32[]{:S(2)}, u32[]{:S(2)}) %collective-permute-start) | collective-permute-done | bytes 524320 | tf_op jit(solution)/shard_map/while/body/eval_jaxpr/ppermute | solution.py:12
  99.2 0.8 copy-done.2
  101.0 1.3 convert_bitcast_fusion.2
  102.4 3.8 %fusion.26 = (f32[64]{0:T(128)S(1)}, f32[64,4096]{1,0:T(8,128)S(1)}) fusion(f32[64]{0:T(128)S(1)} %add_rsqrt_fusion.3, bf16[2,1,128,4096]{3,2,1,0:T(8,128)(2,1)S(1)} %get-tuple-element.368, s32[]{:T(128)S(6)} %select_n.181, s32[]{:T(128)S(6)} %select_n.183, f32[4096]{0:T(1024)S(1)} %bitcast.64, bf16[4096,512]{1,0:T(8,128)(2,1)} %get-tuple-element.369, ...), kind=kOutput, calls=%fused_computation.7.clone.1 | convolution fusion | flops 269746112 | bytes 5849608 | tf_op jit(solution)/shard_map/while/body/eval_jaxpr/dot_general | solution.py:56
  106.3 2.3 fusion.27
  108.6 4.3 %collective-permute-start = (bf16[64,4096]{1,0:T(8,128)(2,1)S(1)}, bf16[64,4096]{1,0:T(8,128)(2,1)S(1)}, u32[]{:S(2)}, u32[]{:S(2)}) collective-permute-start(bf16[64,4096]{1,0:T(8,128)(2,1)S(1)} %get-tuple-element.323), channel_id=1, source_target_pairs={{0,24},{8,0},{16,8},{24,16},{1,25},{9,1},{17,9},{25,17},{2,26},{10... | collective-permute-start | bytes 1572872 | tf_op jit(solution)/shard_map/while/body/eval_jaxpr/ppermute | solution.py:12
  113.0 9.8 %collective-permute-done = bf16[64,4096]{1,0:T(8,128)(2,1)S(1)} collective-permute-done((bf16[64,4096]{1,0:T(8,128)(2,1)S(1)}, bf16[64,4096]{1,0:T(8,128)(2,1)S(1)}, u32[]{:S(2)}, u32[]{:S(2)}) %collective-permute-start) | collective-permute-done | bytes 524320 | tf_op jit(solution)/shard_map/while/body/eval_jaxpr/ppermute | solution.py:12
  122.8 0.8 copy-done.2
  124.5 1.3 convert_bitcast_fusion.2
  126.0 3.8 %fusion.26 = (f32[64]{0:T(128)S(1)}, f32[64,4096]{1,0:T(8,128)S(1)}) fusion(f32[64]{0:T(128)S(1)} %add_rsqrt_fusion.3, bf16[2,1,128,4096]{3,2,1,0:T(8,128)(2,1)S(1)} %get-tuple-element.368, s32[]{:T(128)S(6)} %select_n.181, s32[]{:T(128)S(6)} %select_n.183, f32[4096]{0:T(1024)S(1)} %bitcast.64, bf16[4096,512]{1,0:T(8,128)(2,1)} %get-tuple-element.369, ...), kind=kOutput, calls=%fused_computation.7.clone.1 | convolution fusion | flops 269746112 | bytes 5849608 | tf_op jit(solution)/shard_map/while/body/eval_jaxpr/dot_general | solution.py:56
  129.8 2.3 fusion.27
  132.2 4.3 %collective-permute-start = (bf16[64,4096]{1,0:T(8,128)(2,1)S(1)}, bf16[64,4096]{1,0:T(8,128)(2,1)S(1)}, u32[]{:S(2)}, u32[]{:S(2)}) collective-permute-start(bf16[64,4096]{1,0:T(8,128)(2,1)S(1)} %get-tuple-element.323), channel_id=1, source_target_pairs={{0,24},{8,0},{16,8},{24,16},{1,25},{9,1},{17,9},{25,17},{2,26},{10... | collective-permute-start | bytes 1572872 | tf_op jit(solution)/shard_map/while/body/eval_jaxpr/ppermute | solution.py:12
  136.5 9.0 %collective-permute-done = bf16[64,4096]{1,0:T(8,128)(2,1)S(1)} collective-permute-done((bf16[64,4096]{1,0:T(8,128)(2,1)S(1)}, bf16[64,4096]{1,0:T(8,128)(2,1)S(1)}, u32[]{:S(2)}, u32[]{:S(2)}) %collective-permute-start) | collective-permute-done | bytes 524320 | tf_op jit(solution)/shard_map/while/body/eval_jaxpr/ppermute | solution.py:12
  145.5 0.8 copy-done.2
  147.2 1.3 convert_bitcast_fusion.2
  148.7 3.8 %fusion.26 = (f32[64]{0:T(128)S(1)}, f32[64,4096]{1,0:T(8,128)S(1)}) fusion(f32[64]{0:T(128)S(1)} %add_rsqrt_fusion.3, bf16[2,1,128,4096]{3,2,1,0:T(8,128)(2,1)S(1)} %get-tuple-element.368, s32[]{:T(128)S(6)} %select_n.181, s32[]{:T(128)S(6)} %select_n.183, f32[4096]{0:T(1024)S(1)} %bitcast.64, bf16[4096,512]{1,0:T(8,128)(2,1)} %get-tuple-element.369, ...), kind=kOutput, calls=%fused_computation.7.clone.1 | convolution fusion | flops 269746112 | bytes 5849608 | tf_op jit(solution)/shard_map/while/body/eval_jaxpr/dot_general | solution.py:56
  152.5 2.3 fusion.27
  154.9 4.3 %collective-permute-start = (bf16[64,4096]{1,0:T(8,128)(2,1)S(1)}, bf16[64,4096]{1,0:T(8,128)(2,1)S(1)}, u32[]{:S(2)}, u32[]{:S(2)}) collective-permute-start(bf16[64,4096]{1,0:T(8,128)(2,1)S(1)} %get-tuple-element.323), channel_id=1, source_target_pairs={{0,24},{8,0},{16,8},{24,16},{1,25},{9,1},{17,9},{25,17},{2,26},{10... | collective-permute-start | bytes 1572872 | tf_op jit(solution)/shard_map/while/body/eval_jaxpr/ppermute | solution.py:12
  159.2 8.1 %collective-permute-done = bf16[64,4096]{1,0:T(8,128)(2,1)S(1)} collective-permute-done((bf16[64,4096]{1,0:T(8,128)(2,1)S(1)}, bf16[64,4096]{1,0:T(8,128)(2,1)S(1)}, u32[]{:S(2)}, u32[]{:S(2)}) %collective-permute-start) | collective-permute-done | bytes 524320 | tf_op jit(solution)/shard_map/while/body/eval_jaxpr/ppermute | solution.py:12
  167.3 0.8 copy-done.2
  169.0 1.3 convert_bitcast_fusion.2
  170.5 3.8 %fusion.26 = (f32[64]{0:T(128)S(1)}, f32[64,4096]{1,0:T(8,128)S(1)}) fusion(f32[64]{0:T(128)S(1)} %add_rsqrt_fusion.3, bf16[2,1,128,4096]{3,2,1,0:T(8,128)(2,1)S(1)} %get-tuple-element.368, s32[]{:T(128)S(6)} %select_n.181, s32[]{:T(128)S(6)} %select_n.183, f32[4096]{0:T(1024)S(1)} %bitcast.64, bf16[4096,512]{1,0:T(8,128)(2,1)} %get-tuple-element.369, ...), kind=kOutput, calls=%fused_computation.7.clone.1 | convolution fusion | flops 269746112 | bytes 5849608 | tf_op jit(solution)/shard_map/while/body/eval_jaxpr/dot_general | solution.py:56
  174.3 2.3 fusion.27
  176.7 4.3 %collective-permute-start = (bf16[64,4096]{1,0:T(8,128)(2,1)S(1)}, bf16[64,4096]{1,0:T(8,128)(2,1)S(1)}, u32[]{:S(2)}, u32[]{:S(2)}) collective-permute-start(bf16[64,4096]{1,0:T(8,128)(2,1)S(1)} %get-tuple-element.323), channel_id=1, source_target_pairs={{0,24},{8,0},{16,8},{24,16},{1,25},{9,1},{17,9},{25,17},{2,26},{10... | collective-permute-start | bytes 1572872 | tf_op jit(solution)/shard_map/while/body/eval_jaxpr/ppermute | solution.py:12
  181.0 7.2 %collective-permute-done = bf16[64,4096]{1,0:T(8,128)(2,1)S(1)} collective-permute-done((bf16[64,4096]{1,0:T(8,128)(2,1)S(1)}, bf16[64,4096]{1,0:T(8,128)(2,1)S(1)}, u32[]{:S(2)}, u32[]{:S(2)}) %collective-permute-start) | collective-permute-done | bytes 524320 | tf_op jit(solution)/shard_map/while/body/eval_jaxpr/ppermute | solution.py:12
  188.3 0.8 copy-done.2
  190.0 1.3 convert_bitcast_fusion.2
  191.5 3.8 %fusion.26 = (f32[64]{0:T(128)S(1)}, f32[64,4096]{1,0:T(8,128)S(1)}) fusion(f32[64]{0:T(128)S(1)} %add_rsqrt_fusion.3, bf16[2,1,128,4096]{3,2,1,0:T(8,128)(2,1)S(1)} %get-tuple-element.368, s32[]{:T(128)S(6)} %select_n.181, s32[]{:T(128)S(6)} %select_n.183, f32[4096]{0:T(1024)S(1)} %bitcast.64, bf16[4096,512]{1,0:T(8,128)(2,1)} %get-tuple-element.369, ...), kind=kOutput, calls=%fused_computation.7.clone.1 | convolution fusion | flops 269746112 | bytes 5849608 | tf_op jit(solution)/shard_map/while/body/eval_jaxpr/dot_general | solution.py:56
  195.3 2.3 fusion.27
  197.7 4.3 %collective-permute-start = (bf16[64,4096]{1,0:T(8,128)(2,1)S(1)}, bf16[64,4096]{1,0:T(8,128)(2,1)S(1)}, u32[]{:S(2)}, u32[]{:S(2)}) collective-permute-start(bf16[64,4096]{1,0:T(8,128)(2,1)S(1)} %get-tuple-element.323), channel_id=1, source_target_pairs={{0,24},{8,0},{16,8},{24,16},{1,25},{9,1},{17,9},{25,17},{2,26},{10... | collective-permute-start | bytes 1572872 | tf_op jit(solution)/shard_map/while/body/eval_jaxpr/ppermute | solution.py:12
  202.0 6.6 %collective-permute-done = bf16[64,4096]{1,0:T(8,128)(2,1)S(1)} collective-permute-done((bf16[64,4096]{1,0:T(8,128)(2,1)S(1)}, bf16[64,4096]{1,0:T(8,128)(2,1)S(1)}, u32[]{:S(2)}, u32[]{:S(2)}) %collective-permute-start) | collective-permute-done | bytes 524320 | tf_op jit(solution)/shard_map/while/body/eval_jaxpr/ppermute | solution.py:12
  208.6 0.8 copy-done.2
  210.4 1.3 convert_bitcast_fusion.2
  211.9 3.8 %fusion.26 = (f32[64]{0:T(128)S(1)}, f32[64,4096]{1,0:T(8,128)S(1)}) fusion(f32[64]{0:T(128)S(1)} %add_rsqrt_fusion.3, bf16[2,1,128,4096]{3,2,1,0:T(8,128)(2,1)S(1)} %get-tuple-element.368, s32[]{:T(128)S(6)} %select_n.181, s32[]{:T(128)S(6)} %select_n.183, f32[4096]{0:T(1024)S(1)} %bitcast.64, bf16[4096,512]{1,0:T(8,128)(2,1)} %get-tuple-element.369, ...), kind=kOutput, calls=%fused_computation.7.clone.1 | convolution fusion | flops 269746112 | bytes 5849608 | tf_op jit(solution)/shard_map/while/body/eval_jaxpr/dot_general | solution.py:56
  215.7 2.3 fusion.27
  218.0 4.3 %collective-permute-start = (bf16[64,4096]{1,0:T(8,128)(2,1)S(1)}, bf16[64,4096]{1,0:T(8,128)(2,1)S(1)}, u32[]{:S(2)}, u32[]{:S(2)}) collective-permute-start(bf16[64,4096]{1,0:T(8,128)(2,1)S(1)} %get-tuple-element.323), channel_id=1, source_target_pairs={{0,24},{8,0},{16,8},{24,16},{1,25},{9,1},{17,9},{25,17},{2,26},{10... | collective-permute-start | bytes 1572872 | tf_op jit(solution)/shard_map/while/body/eval_jaxpr/ppermute | solution.py:12
  222.4 6.6 %collective-permute-done = bf16[64,4096]{1,0:T(8,128)(2,1)S(1)} collective-permute-done((bf16[64,4096]{1,0:T(8,128)(2,1)S(1)}, bf16[64,4096]{1,0:T(8,128)(2,1)S(1)}, u32[]{:S(2)}, u32[]{:S(2)}) %collective-permute-start) | collective-permute-done | bytes 524320 | tf_op jit(solution)/shard_map/while/body/eval_jaxpr/ppermute | solution.py:12
  229.0 0.8 copy-done.2
  230.7 1.3 convert_bitcast_fusion.2
  232.2 3.8 %fusion.26 = (f32[64]{0:T(128)S(1)}, f32[64,4096]{1,0:T(8,128)S(1)}) fusion(f32[64]{0:T(128)S(1)} %add_rsqrt_fusion.3, bf16[2,1,128,4096]{3,2,1,0:T(8,128)(2,1)S(1)} %get-tuple-element.368, s32[]{:T(128)S(6)} %select_n.181, s32[]{:T(128)S(6)} %select_n.183, f32[4096]{0:T(1024)S(1)} %bitcast.64, bf16[4096,512]{1,0:T(8,128)(2,1)} %get-tuple-element.369, ...), kind=kOutput, calls=%fused_computation.7.clone.1 | convolution fusion | flops 269746112 | bytes 5849608 | tf_op jit(solution)/shard_map/while/body/eval_jaxpr/dot_general | solution.py:56
  236.1 2.3 fusion.27
  238.4 4.3 %collective-permute-start = (bf16[64,4096]{1,0:T(8,128)(2,1)S(1)}, bf16[64,4096]{1,0:T(8,128)(2,1)S(1)}, u32[]{:S(2)}, u32[]{:S(2)}) collective-permute-start(bf16[64,4096]{1,0:T(8,128)(2,1)S(1)} %get-tuple-element.323), channel_id=1, source_target_pairs={{0,24},{8,0},{16,8},{24,16},{1,25},{9,1},{17,9},{25,17},{2,26},{10... | collective-permute-start | bytes 1572872 | tf_op jit(solution)/shard_map/while/body/eval_jaxpr/ppermute | solution.py:12
  242.7 6.6 %collective-permute-done = bf16[64,4096]{1,0:T(8,128)(2,1)S(1)} collective-permute-done((bf16[64,4096]{1,0:T(8,128)(2,1)S(1)}, bf16[64,4096]{1,0:T(8,128)(2,1)S(1)}, u32[]{:S(2)}, u32[]{:S(2)}) %collective-permute-start) | collective-permute-done | bytes 524320 | tf_op jit(solution)/shard_map/while/body/eval_jaxpr/ppermute | solution.py:12
  249.4 0.8 copy-done.2
  250.2 5.4 %convolution_bitcast_fusion = f32[1,4096,512]{2,1,0:T(8,128)} fusion(bf16[2,128,512]{2,1,0:T(8,128)(2,1)S(1)} %get-tuple-element.231, bf16[2,1,128,4096]{3,2,1,0:T(8,128)(2,1)S(1)} %get-tuple-element.382, f32[2,4096]{1,0:T(2,128)} %bitcast.65, f32[2,128]{1,0:T(2,128)S(1)} %add_rsqrt_fusion.1), kind=kOutput, calls=%fused_computation.21 | convolution fusion | flops 1077936128 | bytes 10781696 | tf_op jit(solution)/shard_map/dot_general | solution.py:84
  255.6 72.6 %reduce-scatter.2.cloned.1.call-done = f32[1,512,512]{2,1,0:T(8,128)} async-done(((f32[1,4096,512]{2,1,0:T(8,128)}), f32[1,512,512]{2,1,0:T(8,128)}) %reduce-scatter.2.cloned.1.call-update) | async-done | bytes 1048592 | tf_op jit(solution)/shard_map/reduce_scatter | solution.py:87
  (123 shorter events, 9.3 us)
Async XLA Ops:
  7.2 42.0 %all-gather.2.cloned.1.call-start = ((), (), s32[]{:S(2)}) async-start(), calls=%async_computation.1 | async-start | bytes 4718592 | tf_op jit(solution)/shard_map/all_gather | solution.py:25
  7.9 320.3 %reduce-scatter.2.cloned.1.call-start = ((), (), s32[]{:S(2)}) async-start(), calls=%async_computation.2 | async-start | bytes 9437184 | tf_op jit(solution)/shard_map/reduce_scatter | solution.py:87
  9.3 42.3 %copy-start = (bf16[2,1,128,4096]{3,2,1,0:T(8,128)(2,1)S(1)}, bf16[2,1,128,4096]{3,2,1,0:T(8,128)(2,1)}, u32[]{:S(2)}) copy-start(bf16[2,1,128,4096]{3,2,1,0:T(8,128)(2,1)} %param.6) | copy-start | bytes 6291460
  54.0 3.8 %copy-start.1 = (bf16[64,4096]{1,0:T(8,128)(2,1)S(1)}, bf16[64,4096]{1,0:T(8,128)(2,1)}, u32[]{:S(2)}) copy-start(bf16[64,4096]{1,0:T(8,128)(2,1)} %get-tuple-element.344) | copy-start | bytes 1572868 | tf_op jit(solution)/shard_map/while
  54.0 3.8 %copy-start.3 = (bf16[128,4096]{1,0:T(8,128)(2,1)S(1)}, bf16[128,4096]{1,0:T(8,128)(2,1)}, u32[]{:S(2)}) copy-start(bf16[128,4096]{1,0:T(8,128)(2,1)} %get-tuple-element.367) | copy-start | bytes 3145732 | tf_op jit(solution)/shard_map/while
  60.2 14.8 %collective-permute-start = (bf16[64,4096]{1,0:T(8,128)(2,1)S(1)}, bf16[64,4096]{1,0:T(8,128)(2,1)S(1)}, u32[]{:S(2)}, u32[]{:S(2)}) collective-permute-start(bf16[64,4096]{1,0:T(8,128)(2,1)S(1)} %get-tuple-element.323), channel_id=1, source_target_pairs={{0,24},{8,0},{16,8},{24,16},{1,25},{9,1},{17,9},{25,17},{2,26},{10... | collective-permute-start | bytes 1572872 | tf_op jit(solution)/shard_map/while/body/eval_jaxpr/ppermute | solution.py:12
  75.0 0.8 copy-start.2
  78.2 3.8 %copy-start.1 = (bf16[64,4096]{1,0:T(8,128)(2,1)S(1)}, bf16[64,4096]{1,0:T(8,128)(2,1)}, u32[]{:S(2)}) copy-start(bf16[64,4096]{1,0:T(8,128)(2,1)} %get-tuple-element.344) | copy-start | bytes 1572868 | tf_op jit(solution)/shard_map/while
  78.2 3.8 %copy-start.3 = (bf16[128,4096]{1,0:T(8,128)(2,1)S(1)}, bf16[128,4096]{1,0:T(8,128)(2,1)}, u32[]{:S(2)}) copy-start(bf16[128,4096]{1,0:T(8,128)(2,1)} %get-tuple-element.367) | copy-start | bytes 3145732 | tf_op jit(solution)/shard_map/while
  84.4 14.9 %collective-permute-start = (bf16[64,4096]{1,0:T(8,128)(2,1)S(1)}, bf16[64,4096]{1,0:T(8,128)(2,1)S(1)}, u32[]{:S(2)}, u32[]{:S(2)}) collective-permute-start(bf16[64,4096]{1,0:T(8,128)(2,1)S(1)} %get-tuple-element.323), channel_id=1, source_target_pairs={{0,24},{8,0},{16,8},{24,16},{1,25},{9,1},{17,9},{25,17},{2,26},{10... | collective-permute-start | bytes 1572872 | tf_op jit(solution)/shard_map/while/body/eval_jaxpr/ppermute | solution.py:12
  99.2 0.8 copy-start.2
  102.4 3.8 %copy-start.1 = (bf16[64,4096]{1,0:T(8,128)(2,1)S(1)}, bf16[64,4096]{1,0:T(8,128)(2,1)}, u32[]{:S(2)}) copy-start(bf16[64,4096]{1,0:T(8,128)(2,1)} %get-tuple-element.344) | copy-start | bytes 1572868 | tf_op jit(solution)/shard_map/while
  102.4 3.8 %copy-start.3 = (bf16[128,4096]{1,0:T(8,128)(2,1)S(1)}, bf16[128,4096]{1,0:T(8,128)(2,1)}, u32[]{:S(2)}) copy-start(bf16[128,4096]{1,0:T(8,128)(2,1)} %get-tuple-element.367) | copy-start | bytes 3145732 | tf_op jit(solution)/shard_map/while
  108.6 14.2 %collective-permute-start = (bf16[64,4096]{1,0:T(8,128)(2,1)S(1)}, bf16[64,4096]{1,0:T(8,128)(2,1)S(1)}, u32[]{:S(2)}, u32[]{:S(2)}) collective-permute-start(bf16[64,4096]{1,0:T(8,128)(2,1)S(1)} %get-tuple-element.323), channel_id=1, source_target_pairs={{0,24},{8,0},{16,8},{24,16},{1,25},{9,1},{17,9},{25,17},{2,26},{10... | collective-permute-start | bytes 1572872 | tf_op jit(solution)/shard_map/while/body/eval_jaxpr/ppermute | solution.py:12
  122.8 0.8 copy-start.2
  126.0 3.8 %copy-start.1 = (bf16[64,4096]{1,0:T(8,128)(2,1)S(1)}, bf16[64,4096]{1,0:T(8,128)(2,1)}, u32[]{:S(2)}) copy-start(bf16[64,4096]{1,0:T(8,128)(2,1)} %get-tuple-element.344) | copy-start | bytes 1572868 | tf_op jit(solution)/shard_map/while
  126.0 3.8 %copy-start.3 = (bf16[128,4096]{1,0:T(8,128)(2,1)S(1)}, bf16[128,4096]{1,0:T(8,128)(2,1)}, u32[]{:S(2)}) copy-start(bf16[128,4096]{1,0:T(8,128)(2,1)} %get-tuple-element.367) | copy-start | bytes 3145732 | tf_op jit(solution)/shard_map/while
  132.2 13.3 %collective-permute-start = (bf16[64,4096]{1,0:T(8,128)(2,1)S(1)}, bf16[64,4096]{1,0:T(8,128)(2,1)S(1)}, u32[]{:S(2)}, u32[]{:S(2)}) collective-permute-start(bf16[64,4096]{1,0:T(8,128)(2,1)S(1)} %get-tuple-element.323), channel_id=1, source_target_pairs={{0,24},{8,0},{16,8},{24,16},{1,25},{9,1},{17,9},{25,17},{2,26},{10... | collective-permute-start | bytes 1572872 | tf_op jit(solution)/shard_map/while/body/eval_jaxpr/ppermute | solution.py:12
  145.5 0.8 copy-start.2
  148.7 3.8 %copy-start.1 = (bf16[64,4096]{1,0:T(8,128)(2,1)S(1)}, bf16[64,4096]{1,0:T(8,128)(2,1)}, u32[]{:S(2)}) copy-start(bf16[64,4096]{1,0:T(8,128)(2,1)} %get-tuple-element.344) | copy-start | bytes 1572868 | tf_op jit(solution)/shard_map/while
  148.7 3.8 %copy-start.3 = (bf16[128,4096]{1,0:T(8,128)(2,1)S(1)}, bf16[128,4096]{1,0:T(8,128)(2,1)}, u32[]{:S(2)}) copy-start(bf16[128,4096]{1,0:T(8,128)(2,1)} %get-tuple-element.367) | copy-start | bytes 3145732 | tf_op jit(solution)/shard_map/while
  154.9 12.4 %collective-permute-start = (bf16[64,4096]{1,0:T(8,128)(2,1)S(1)}, bf16[64,4096]{1,0:T(8,128)(2,1)S(1)}, u32[]{:S(2)}, u32[]{:S(2)}) collective-permute-start(bf16[64,4096]{1,0:T(8,128)(2,1)S(1)} %get-tuple-element.323), channel_id=1, source_target_pairs={{0,24},{8,0},{16,8},{24,16},{1,25},{9,1},{17,9},{25,17},{2,26},{10... | collective-permute-start | bytes 1572872 | tf_op jit(solution)/shard_map/while/body/eval_jaxpr/ppermute | solution.py:12
  167.3 0.8 copy-start.2
  170.5 3.8 %copy-start.1 = (bf16[64,4096]{1,0:T(8,128)(2,1)S(1)}, bf16[64,4096]{1,0:T(8,128)(2,1)}, u32[]{:S(2)}) copy-start(bf16[64,4096]{1,0:T(8,128)(2,1)} %get-tuple-element.344) | copy-start | bytes 1572868 | tf_op jit(solution)/shard_map/while
  170.5 3.8 %copy-start.3 = (bf16[128,4096]{1,0:T(8,128)(2,1)S(1)}, bf16[128,4096]{1,0:T(8,128)(2,1)}, u32[]{:S(2)}) copy-start(bf16[128,4096]{1,0:T(8,128)(2,1)} %get-tuple-element.367) | copy-start | bytes 3145732 | tf_op jit(solution)/shard_map/while
  176.7 11.6 %collective-permute-start = (bf16[64,4096]{1,0:T(8,128)(2,1)S(1)}, bf16[64,4096]{1,0:T(8,128)(2,1)S(1)}, u32[]{:S(2)}, u32[]{:S(2)}) collective-permute-start(bf16[64,4096]{1,0:T(8,128)(2,1)S(1)} %get-tuple-element.323), channel_id=1, source_target_pairs={{0,24},{8,0},{16,8},{24,16},{1,25},{9,1},{17,9},{25,17},{2,26},{10... | collective-permute-start | bytes 1572872 | tf_op jit(solution)/shard_map/while/body/eval_jaxpr/ppermute | solution.py:12
  188.3 0.8 copy-start.2
  191.5 3.8 %copy-start.1 = (bf16[64,4096]{1,0:T(8,128)(2,1)S(1)}, bf16[64,4096]{1,0:T(8,128)(2,1)}, u32[]{:S(2)}) copy-start(bf16[64,4096]{1,0:T(8,128)(2,1)} %get-tuple-element.344) | copy-start | bytes 1572868 | tf_op jit(solution)/shard_map/while
  191.5 3.8 %copy-start.3 = (bf16[128,4096]{1,0:T(8,128)(2,1)S(1)}, bf16[128,4096]{1,0:T(8,128)(2,1)}, u32[]{:S(2)}) copy-start(bf16[128,4096]{1,0:T(8,128)(2,1)} %get-tuple-element.367) | copy-start | bytes 3145732 | tf_op jit(solution)/shard_map/while
  197.7 11.0 %collective-permute-start = (bf16[64,4096]{1,0:T(8,128)(2,1)S(1)}, bf16[64,4096]{1,0:T(8,128)(2,1)S(1)}, u32[]{:S(2)}, u32[]{:S(2)}) collective-permute-start(bf16[64,4096]{1,0:T(8,128)(2,1)S(1)} %get-tuple-element.323), channel_id=1, source_target_pairs={{0,24},{8,0},{16,8},{24,16},{1,25},{9,1},{17,9},{25,17},{2,26},{10... | collective-permute-start | bytes 1572872 | tf_op jit(solution)/shard_map/while/body/eval_jaxpr/ppermute | solution.py:12
  208.6 0.8 copy-start.2
  211.8 3.8 %copy-start.1 = (bf16[64,4096]{1,0:T(8,128)(2,1)S(1)}, bf16[64,4096]{1,0:T(8,128)(2,1)}, u32[]{:S(2)}) copy-start(bf16[64,4096]{1,0:T(8,128)(2,1)} %get-tuple-element.344) | copy-start | bytes 1572868 | tf_op jit(solution)/shard_map/while
  211.8 3.8 %copy-start.3 = (bf16[128,4096]{1,0:T(8,128)(2,1)S(1)}, bf16[128,4096]{1,0:T(8,128)(2,1)}, u32[]{:S(2)}) copy-start(bf16[128,4096]{1,0:T(8,128)(2,1)} %get-tuple-element.367) | copy-start | bytes 3145732 | tf_op jit(solution)/shard_map/while
  218.0 11.0 %collective-permute-start = (bf16[64,4096]{1,0:T(8,128)(2,1)S(1)}, bf16[64,4096]{1,0:T(8,128)(2,1)S(1)}, u32[]{:S(2)}, u32[]{:S(2)}) collective-permute-start(bf16[64,4096]{1,0:T(8,128)(2,1)S(1)} %get-tuple-element.323), channel_id=1, source_target_pairs={{0,24},{8,0},{16,8},{24,16},{1,25},{9,1},{17,9},{25,17},{2,26},{10... | collective-permute-start | bytes 1572872 | tf_op jit(solution)/shard_map/while/body/eval_jaxpr/ppermute | solution.py:12
  229.0 0.8 copy-start.2
  232.2 3.8 %copy-start.1 = (bf16[64,4096]{1,0:T(8,128)(2,1)S(1)}, bf16[64,4096]{1,0:T(8,128)(2,1)}, u32[]{:S(2)}) copy-start(bf16[64,4096]{1,0:T(8,128)(2,1)} %get-tuple-element.344) | copy-start | bytes 1572868 | tf_op jit(solution)/shard_map/while
  232.2 3.8 %copy-start.3 = (bf16[128,4096]{1,0:T(8,128)(2,1)S(1)}, bf16[128,4096]{1,0:T(8,128)(2,1)}, u32[]{:S(2)}) copy-start(bf16[128,4096]{1,0:T(8,128)(2,1)} %get-tuple-element.367) | copy-start | bytes 3145732 | tf_op jit(solution)/shard_map/while
  238.4 11.0 %collective-permute-start = (bf16[64,4096]{1,0:T(8,128)(2,1)S(1)}, bf16[64,4096]{1,0:T(8,128)(2,1)S(1)}, u32[]{:S(2)}, u32[]{:S(2)}) collective-permute-start(bf16[64,4096]{1,0:T(8,128)(2,1)S(1)} %get-tuple-element.323), channel_id=1, source_target_pairs={{0,24},{8,0},{16,8},{24,16},{1,25},{9,1},{17,9},{25,17},{2,26},{10... | collective-permute-start | bytes 1572872 | tf_op jit(solution)/shard_map/while/body/eval_jaxpr/ppermute | solution.py:12
  249.4 0.8 copy-start.2
Sparse Core Ops, SparseCore 0:
  9.9 39.2 all-gather.1
  255.7 72.4 reduce-scatter.1
where the time goes:
time: 336 us; the launch traced here: 335 us
  waiting for transfers between devices  187 us (56%)
  matrix products  39.5 us (12%)
  other arithmetic  38.2 us (11%)
  starting transfers between devices  37.3 us (11%)
  local copies, waits for them, and re-layouts  18.1 us (5%)
  between operations  14 us (4%)
    ppermute x9, waiting for transfers between devices, passed_along(): return lax.ppermute(value, axis, pairs)  76.2 us
    reduce_scatter x1, waiting for transfers between devices, on_device(): lax.psum_scatter(full_grad[None], 'dp', scatter_dimension=1, tiled=True)  72.6 us
    all_gather x1, waiting for transfers between devices, on_device(): w_full = lax.all_gather(w_value, 'dp', axis=1, tiled=True)  37.6 us
    ppermute x9, starting transfers between devices, passed_along(): return lax.ppermute(value, axis, pairs)  37.2 us
    dot_general x9, matrix products, one_step(): lax.dot_general(dv, w_mat, (((1,), (1,)), ((), ())), preferred_element_ty...  34.2 us
    dynamic_update_slice x9, other arithmetic, one_step(): lax.dynamic_update_slice(grad_buf, jnp.where(valid, dx[None], old_x), (lo...  21.1 us
    while x18, other arithmetic  12.6 us
    while x63, local copies, waits for them, and re-layouts  7.48 us
  transfers between devices with their start and end apart: 11, of which 11 were waited for; matrix products, arithmetic and copies ran while one was open for 1% of the time, Pallas kernels for 0%

commit v1 on v0

v1 whole, which is shorter than its diff:
```python
import functools

import jax
import jax.numpy as jnp
from jax import lax
from jax.experimental import pallas as pl
from jax.experimental.pallas import tpu as pltpu
from jax.sharding import PartitionSpec as P

HEAD = 128
BLOCKS = 2
CHUNKS = 8
EARLY = 6
MESH = pl.DeviceIdType.MESH
F32 = jnp.float32
BF16 = jnp.bfloat16


def kernel(
    npipe, ndp,
    x_ref, go_ref, g_ref, w_ref, gx_ref, gw_ref,
    wfull, ht, hall, dvall, vcur, vsend, cbuf, dhg, rinv,
    s1r, s0r, p1r, s1s, s0s, p1s,
    w_send, w_recv, f_send, f_recv, h_send, h_recv, d_send, d_recv,
    v_send, v_recv, s1_ss, s1_rs, s0_ss, s0_rs, p1_ss, p1_rs, loc,
):
    p = lax.axis_index("pipe")
    me = lax.axis_index("dp")
    tok, width = go_ref.shape
    kv = w_ref.shape[1]
    shard = w_ref.shape[0]
    group = width // kv
    tile = group * HEAD
    heads = kv // HEAD
    half = ndp // 2
    chip = me // 2
    core = me % 2
    sib = 2 * chip + 1 - core
    below = (p + npipe - 1) % npipe
    above = (p + 1) % npipe
    brow = tok // BLOCKS
    crow = tok // CHUNKS
    last = p == npipe - 1
    first = p == 0

    def remote(src, dst, ss, rs, pipe, dp):
        return pltpu.make_async_remote_copy(
            src_ref=src, dst_ref=dst, send_sem=ss, recv_sem=rs,
            device_id=(pipe, dp), device_id_type=MESH,
        )

    barrier = pltpu.get_barrier_semaphore()

    def greet(j, _):
        pl.semaphore_signal(
            barrier, inc=1, device_id=(p, (me + j) % ndp), device_id_type=MESH
        )
        return 0

    lax.fori_loop(1, ndp, greet, 0)
    pl.semaphore_signal(barrier, inc=1, device_id=(below, me), device_id_type=MESH)
    pl.semaphore_signal(barrier, inc=1, device_id=(above, me), device_id_type=MESH)
    pl.semaphore_wait(barrier, ndp + 1)

    def wrows(owner):
        return wfull.at[pl.ds(pl.multiple_of(owner * shard, shard), shard)]

    def w_copy(j):
        peer = 2 * ((chip + j) % half) + core
        return remote(w_ref, wrows(me), w_send.at[j], w_recv.at[j], p, peer)

    def f_copy(j):
        owner = 2 * ((chip + half - j) % half) + core
        return remote(wrows(owner), wrows(owner), f_send.at[j], f_recv.at[j], p, sib)

    f_own = remote(w_ref, wrows(me), f_send.at[0], f_recv.at[0], p, sib)

    def start_w(j, _):
        w_copy(j).start()
        return 0

    lax.fori_loop(1, half, start_w, 0)
    f_own.start()
    own_w = pltpu.make_async_copy(w_ref, wrows(me), loc.at[0])
    own_w.start()

    @pl.when(last)
    def _():
        s1r[...] = jnp.zeros_like(s1r)
        s0r[...] = jnp.zeros_like(s0r)
        for t in range(heads):
            acc = go_ref[:, t * tile:t * tile + HEAD].astype(F32)
            for r in range(1, group):
                lo = t * tile + r * HEAD
                acc = acc + go_ref[:, lo:lo + HEAD].astype(F32)
            vcur[1, :, t * HEAD:(t + 1) * HEAD] = acc.astype(BF16)

    @pl.when(first)
    def _():
        p1r[...] = jnp.zeros_like(p1r)

    for l in range(2):
        total = jnp.zeros((tok, HEAD), F32)
        for t in range(width // HEAD):
            xx = x_ref[l, :, t * HEAD:(t + 1) * HEAD].astype(F32)
            total = total + xx * xx
        mean = jnp.sum(total, axis=-1, keepdims=True) / width
        rinv[l] = jnp.broadcast_to(lax.rsqrt(mean + 1e-05), (tok, HEAD))
        for t in range(width // HEAD):
            cols = slice(t * HEAD, (t + 1) * HEAD)
            xn = x_ref[l, :, cols].astype(F32) * rinv[l]
            hid = xn * g_ref[l:l + 1, cols]
            ht[cols, l * tok:(l + 1) * tok] = hid.T.astype(BF16)

    def hrows(owner):
        return ht.at[pl.ds(pl.multiple_of(owner * shard, shard), shard)]

    wide = 2 * tok
    hslot = hall.at[:, pl.ds(pl.multiple_of(me * wide, wide), wide)]

    def h_copy(j):
        peer = (me + j) % ndp
        return remote(hrows(peer), hslot, h_send.at[j], h_recv.at[j], p, peer)

    def start_h(j, _):
        h_copy(j).start()
        return 0

    lax.fori_loop(1, ndp, start_h, 0)
    own_h = pltpu.make_async_copy(hrows(me), hslot, loc.at[1])
    own_h.start()

    def forward_w(j, _):
        w_copy(j).wait_recv()
        f_copy(j).start()
        return 0

    lax.fori_loop(1, half, forward_w, 0)
    own_w.wait()
    f_own.wait_recv()

    def arrived_w(j, _):
        f_copy(j).wait_recv()
        return 0

    lax.fori_loop(1, half, arrived_w, 0)

    def d_slot(l):
        return dvall.at[pl.ds(pl.multiple_of((me * 2 + l) * tok, tok), tok)]

    def d_copy(l, j):
        peer = (me + j) % ndp
        return remote(
            vcur.at[l], d_slot(l), d_send.at[l, j], d_recv.at[l, j], p, peer
        )

    def v_copy(l, b):
        slot = l - (npipe - 1 - p) // (npipe - 1)
        rows = pl.ds(b * brow, brow)
        return remote(
            vsend.at[l, rows], vcur.at[slot, rows],
            v_send.at[l, b], v_recv.at[slot, b], below, me,
        )

    def v_arrival(l, b):
        rows = pl.ds(b * brow, brow)
        return remote(
            vsend.at[l, rows], vcur.at[l, rows],
            v_send.at[l, b], v_recv.at[l, b], below, me,
        )

    def turn(l):
        for b in range(BLOCKS):
            rows = slice(b * brow, (b + 1) * brow)
            if l == 1:
                @pl.when(jnp.logical_not(last))
                def _():
                    v_arrival(l, b).wait_recv()
            else:
                v_arrival(l, b).wait_recv()
            vb = vcur[l, rows]
            ri = rinv[l, rows]
            total = jnp.zeros((brow, HEAD), F32)
            for t in range(heads):
                dh = lax.dot_general(
                    vb, wfull[t * tile:(t + 1) * tile],
                    (((1,), (1,)), ((), ())), preferred_element_type=F32,
                )
                for r in range(group):
                    cols = slice(t * tile + r * HEAD, t * tile + (r + 1) * HEAD)
                    d = dh[:, r * HEAD:(r + 1) * HEAD] * g_ref[l:l + 1, cols]
                    dhg[:, cols] = d
                    total = total + d * (x_ref[l, rows, cols].astype(F32) * ri)
            mean = jnp.sum(total, axis=-1, keepdims=True) / width
            for t in range(heads):
                acc = vb[:, t * HEAD:(t + 1) * HEAD].astype(F32)
                for r in range(group):
                    cols = slice(t * tile + r * HEAD, t * tile + (r + 1) * HEAD)
                    xn = x_ref[l, rows, cols].astype(F32) * ri
                    c = ri * (dhg[:, cols] - xn * mean)
                    cbuf[l, rows, cols] = c
                    acc = acc + c
                vsend[l, rows, t * HEAD:(t + 1) * HEAD] = acc.astype(BF16)
            if l == 1:
                v_copy(l, b).start()
            else:
                @pl.when(jnp.logical_not(first))
                def _():
                    v_copy(l, b).start()

        def start_d(j, _):
            d_copy(l, j).start()
            return 0

        lax.fori_loop(1, ndp, start_d, 0)
        own = pltpu.make_async_copy(vcur.at[l], d_slot(l), loc.at[2 + l])
        own.start()
        return own

    def crows(i):
        return pl.ds(pl.multiple_of(i * crow, crow), crow)

    def s1_copy(i):
        r = crows(i)
        return remote(s1s.at[r], s1r.at[r], s1_ss.at[i], s1_rs.at[i], below, me)

    def s0_copy(i):
        r = crows(i)
        return remote(s0s.at[r], s0r.at[r], s0_ss.at[i], s0_rs.at[i], below, me)

    def p1_copy(i):
        r = crows(i)
        return remote(p1s.at[r], p1r.at[r], p1_ss.at[i], p1_rs.at[i], above, me)

    def relay_s1(i, _):
        @pl.when(jnp.logical_not(last))
        def _():
            s1_copy(i).wait_recv()
        r = crows(i)
        s1 = cbuf[1, r] + s1r[r].astype(F32)
        s1s[r] = s1.astype(BF16)

        @pl.when(jnp.logical_not(first))
        def _():
            s1_copy(i).start()
        gx_ref[1, r] = (go_ref[r].astype(F32) + s1).astype(BF16)
        return 0

    def start_p1(i, _):
        r = crows(i)
        p1s[r] = cbuf[1, r].astype(BF16)
        p1_copy(i).start()
        return 0

    own_d1 = turn(1)

    @pl.when(first)
    def _():
        lax.fori_loop(0, CHUNKS, start_p1, 0)

    lax.fori_loop(0, EARLY, relay_s1, 0)

    @pl.when(last)
    def _():
        lax.fori_loop(EARLY, CHUNKS, relay_s1, 0)

    own_d0 = turn(0)

    @pl.when(jnp.logical_not(last))
    def _():
        lax.fori_loop(EARLY, CHUNKS, relay_s1, 0)

    def relay_rest(i, _):
        r = crows(i)

        @pl.when(jnp.logical_not(last))
        def _():
            s0_copy(i).wait_recv()
        s0 = cbuf[0, r] + s0r[r].astype(F32)

        @pl.when(jnp.logical_not(first))
        def _():
            s0s[r] = s0.astype(BF16)
            s0_copy(i).start()
        cbuf[0, r] = s0

        @pl.when(jnp.logical_not(first) & jnp.logical_not(last))
        def _():
            p1_copy(i).wait_recv()
            p1s[r] = (cbuf[1, r] + p1r[r].astype(F32)).astype(BF16)
            p1_copy(i).start()
        return 0

    def finish(i, _):
        r = crows(i)

        @pl.when(last)
        def _():
            p1_copy(i).wait_recv()
        dy = go_ref[r].astype(F32) + (cbuf[1, r] + s1r[r].astype(F32))
        gx_ref[0, r] = (dy + p1r[r].astype(F32) + cbuf[0, r]).astype(BF16)
        return 0

    lax.fori_loop(0, CHUNKS, relay_rest, 0)

    def arrived_h(j, _):
        h_copy(j).wait_recv()
        d_copy(0, j).wait_recv()
        d_copy(1, j).wait_recv()
        return 0

    lax.fori_loop(1, ndp, arrived_h, 0)
    own_h.wait()
    own_d1.wait()
    own_d0.wait()
    depth = ndp * wide
    step = min(depth, 2048)

    def product(k):
        cols = pl.ds(pl.multiple_of(k * step, step), step)
        return jnp.dot(hall[:, cols], dvall[cols], preferred_element_type=F32)

    gw_ref[...] = product(0)

    def more(k, _):
        gw_ref[...] += product(k)
        return 0

    if depth > step:
        lax.fori_loop(1, depth // step, more, 0)

    lax.fori_loop(0, CHUNKS, finish, 0)

    def sent_w(j, _):
        w_copy(j).wait_send()
        f_copy(j).wait_send()
        return 0

    lax.fori_loop(1, half, sent_w, 0)
    f_own.wait_send()

    def sent_h(j, _):
        h_copy(j).wait_send()
        d_copy(0, j).wait_send()
        d_copy(1, j).wait_send()
        return 0

    lax.fori_loop(1, ndp, sent_h, 0)
    for b in range(BLOCKS):
        v_copy(1, b).wait_send()

    def sent_s(i, _):
        s1_copy(i).wait_send()
        s0_copy(i).wait_send()
        return 0

    def sent_p(i, _):
        p1_copy(i).wait_send()
        return 0

    @pl.when(jnp.logical_not(first))
    def _():
        for b in range(BLOCKS):
            v_copy(0, b).wait_send()
        lax.fori_loop(0, CHUNKS, sent_s, 0)

    @pl.when(jnp.logical_not(last))
    def _():
        lax.fori_loop(0, CHUNKS, sent_p, 0)


def on_device(saved, grad_out, gain, w_value):
    npipe = lax.axis_size("pipe")
    ndp = lax.axis_size("dp")
    tok, width = grad_out.shape
    shard, kv = w_value.shape[1:]
    wide = 2 * tok
    dma = pltpu.SemaphoreType.DMA
    vmem = pl.BlockSpec(memory_space=pltpu.VMEM)
    gx, gw = pl.pallas_call(
        functools.partial(kernel, npipe, ndp),
        out_shape=(
            jax.ShapeDtypeStruct((2, tok, width), BF16),
            jax.ShapeDtypeStruct((shard, kv), F32),
        ),
        in_specs=[vmem] * 4,
        out_specs=(vmem, vmem),
        scratch_shapes=[
            pltpu.VMEM((width, kv), BF16),
            pltpu.VMEM((width, wide), BF16),
            pltpu.VMEM((shard, ndp * wide), BF16),
            pltpu.VMEM((ndp * wide, kv), BF16),
            pltpu.VMEM((2, tok, kv), BF16),
            pltpu.VMEM((2, tok, kv), BF16),
            pltpu.VMEM((2, tok, width), F32),
            pltpu.VMEM((tok // BLOCKS, width), F32),
            pltpu.VMEM((2, tok, HEAD), F32),
        ]
        + [pltpu.VMEM((tok, width), BF16)] * 6
        + [dma((ndp,))] * 6
        + [dma((2, ndp))] * 2
        + [dma((2, BLOCKS))] * 2
        + [dma((CHUNKS,))] * 6
        + [dma((4,))],
        compiler_params=pltpu.CompilerParams(
            collective_id=0, has_side_effects=True, vmem_limit_bytes=60 * 1024 * 1024
        ),
    )(saved[:, 0], grad_out, gain[:, 0], w_value[0])
    return gx[:, None], gw[None]


def solution(mesh):
    return jax.shard_map(
        on_device,
        mesh=mesh,
        in_specs=(
            P(None, "pipe", "dp", None),
            P("dp", None),
            P(None, "pipe", None),
            P("pipe", "dp", None),
        ),
        out_specs=(P(None, "pipe", "dp", None), P("pipe", "dp", None)),
        check_vma=False,
    )
```

time: 336 us -> 155 us (0.46)
  waiting for transfers between devices: 187 us -> 0 us
  Pallas kernels: 0 us -> 149 us
  matrix products: 39.5 us -> 0 us
  other arithmetic: 38.2 us -> 0 us
  starting transfers between devices: 37.3 us -> 0 us
  between operations: 14 us -> 0.65 us
  local copies, waits for them, and re-layouts: 18.1 us -> 5.59 us
    pallas_call x0 -> x1, Pallas kernels: none -> 149 us  [on_device(): pl.pallas_call(functools.partial(kernel, npipe, ndp), out_shape=(jax.Shap...]
    ppermute x9 -> x0, waiting for transfers between devices: 76.2 us -> none  [passed_along(): return lax.ppermute(value, axis, pairs)]
    reduce_scatter x1 -> x0, waiting for transfers between devices: 72.6 us -> none  [on_device(): lax.psum_scatter(full_grad[None], 'dp', scatter_dimension=1, tiled=True)]
    dot_general x10 -> x0, matrix products: 39.5 us -> none  [the longest x9 34.2 us: one_step(): lax.dot_general(dv, w_mat, (((1,), (1,)), ((), ())), preferred_element_ty...]
    all_gather x1 -> x0, waiting for transfers between devices: 37.6 us -> none  [on_device(): w_full = lax.all_gather(w_value, 'dp', axis=1, tiled=True)]
    ppermute x9 -> x0, starting transfers between devices: 37.2 us -> none  [passed_along(): return lax.ppermute(value, axis, pairs)]
    dynamic_update_slice x18 -> x0, other arithmetic: 21.3 us -> none  [the longest x9 21.1 us: one_step(): lax.dynamic_update_slice(grad_buf, jnp.where(valid, dx[None], old_x), (lo...]
    while x18 -> x0, other arithmetic: 12.6 us -> none
  transfers between devices with their start and end apart: 11 -> 0, of which waited for: 11 -> 0; matrix products, arithmetic and copies ran while one was open for 1% -> 0% of each run, Pallas kernels for 0% -> 0%
where the time goes in v1:
time: 155 us
  Pallas kernels  149 us (96%)
  local copies, waits for them, and re-layouts  5.59 us (4%)
    pallas_call x1, Pallas kernels, on_device(): pl.pallas_call(functools.partial(kernel, npipe, ndp), out_shape=(jax.Shap...  149 us
    unnamed x5, local copies, waits for them, and re-layouts  5.59 us

profile of v1, /device:TPU:0, one launch (start us, length us, event | category | flops | bytes accessed | tf_op | source)
XLA Modules:
  0.0 154.9 jit_solution(13255705081924420993)
XLA Ops:
  0.6 1.4 copy.9
  2.0 148.7 %shard_map.59 = (bf16[2,128,4096]{2,1,0:T(8,128)(2,1)}, f32[512,512]{1,0:T(8,128)}) custom-call(bf16[2,128,4096]{2,1,0:T(8,128)(2,1)} %bitcast.9, bf16[128,4096]{1,0:T(8,128)(2,1)} %go_ref.1, f32[2,4096]{1,0:T(2,128)} %bitcast.13, bf16[512,512]{1,0:T(8,128)(2,1)} %bitcast.12), custom_call_target="tpu_custom_call" | custom-call | tf_op jit(solution)/shard_map/pallas_call | solution.py:380
  150.7 0.0 copy-start
  150.7 3.2 %copy.12 = bf16[2,1,128,4096]{3,2,1,0:T(8,128)(2,1)} copy(bf16[2,1,128,4096]{3,2,1,0:T(8,128)(2,1)} %bitcast.10) | data formatting | bytes 4194304
  154.0 0.0 copy-done
  154.0 1.0 copy.13
Async XLA Ops:
  150.7 3.2 %copy-start = (f32[512,512]{1,0:T(8,128)S(1)}, f32[512,512]{1,0:T(8,128)}, u32[]{:S(2)}) copy-start(f32[512,512]{1,0:T(8,128)} %get-tuple-element.5) | copy-start | bytes 3145732

commit v2 on v1

--- a/solution.py
+++ b/solution.py
@@ -11,6 +11,7 @@
 BLOCKS = 2
 CHUNKS = 8
 EARLY = 6
+AHEAD = 3
 MESH = pl.DeviceIdType.MESH
 F32 = jnp.float32
 BF16 = jnp.bfloat16
@@ -270,7 +271,7 @@
     def _():
         lax.fori_loop(EARLY, CHUNKS, relay_s1, 0)
 
-    def relay_rest(i, _):
+    def relay_s0(i, _):
         r = crows(i)
 
         @pl.when(jnp.logical_not(last))
@@ -283,6 +284,10 @@
             s0s[r] = s0.astype(BF16)
             s0_copy(i).start()
         cbuf[0, r] = s0
+        return 0
+
+    def relay_p1(i, _):
+        r = crows(i)
 
         @pl.when(jnp.logical_not(first) & jnp.logical_not(last))
         def _():
@@ -291,6 +296,10 @@
             p1_copy(i).start()
         return 0
 
+    def relay_both(i, _):
+        relay_p1(i + AHEAD, 0)
+        return relay_s0(i, 0)
+
     def finish(i, _):
         r = crows(i)
 
@@ -301,7 +310,9 @@
         gx_ref[0, r] = (dy + p1r[r].astype(F32) + cbuf[0, r]).astype(BF16)
         return 0
 
-    lax.fori_loop(0, CHUNKS, relay_rest, 0)
+    lax.fori_loop(0, AHEAD, relay_p1, 0)
+    lax.fori_loop(0, CHUNKS - AHEAD, relay_both, 0)
+    lax.fori_loop(CHUNKS - AHEAD, CHUNKS, relay_s0, 0)
 
     def arrived_h(j, _):
         h_copy(j).wait_recv()

time: 155 us -> 149 us (0.961)
  Pallas kernels: 149 us -> 143 us
    pallas_call x1, Pallas kernels: 149 us -> 143 us  [on_device(): pl.pallas_call(functools.partial(kernel, npipe, ndp), out_shape=(jax.Shap...]
where the time goes in v2:
time: 149 us
  Pallas kernels  143 us (96%)
  local copies, waits for them, and re-layouts  5.59 us (4%)
    pallas_call x1, Pallas kernels, on_device(): pl.pallas_call(functools.partial(kernel, npipe, ndp), out_shape=(jax.Shap...  143 us
    unnamed x5, local copies, waits for them, and re-layouts  5.59 us

profile of v2, /device:TPU:0, one launch (start us, length us, event | category | flops | bytes accessed | tf_op | source)
XLA Modules:
  0.0 149.0 jit_solution(10175894435647544611)
XLA Ops:
  0.6 1.4 copy.9
  2.0 142.7 %shard_map.59 = (bf16[2,128,4096]{2,1,0:T(8,128)(2,1)}, f32[512,512]{1,0:T(8,128)}) custom-call(bf16[2,128,4096]{2,1,0:T(8,128)(2,1)} %bitcast.9, bf16[128,4096]{1,0:T(8,128)(2,1)} %go_ref.1, f32[2,4096]{1,0:T(2,128)} %bitcast.13, bf16[512,512]{1,0:T(8,128)(2,1)} %bitcast.12), custom_call_target="tpu_custom_call" | custom-call | tf_op jit(solution)/shard_map/pallas_call | solution.py:391
  144.8 0.0 copy-start
  144.8 3.2 %copy.12 = bf16[2,1,128,4096]{3,2,1,0:T(8,128)(2,1)} copy(bf16[2,1,128,4096]{3,2,1,0:T(8,128)(2,1)} %bitcast.10) | data formatting | bytes 4194304
  148.0 0.0 copy-done
  148.0 1.0 copy.13
Async XLA Ops:
  144.8 3.2 %copy-start = (f32[512,512]{1,0:T(8,128)S(1)}, f32[512,512]{1,0:T(8,128)}, u32[]{:S(2)}) copy-start(f32[512,512]{1,0:T(8,128)} %get-tuple-element.5) | copy-start | bytes 3145732

commit v3 on v2

--- a/solution.py
+++ b/solution.py
@@ -10,7 +10,8 @@
 HEAD = 128
 BLOCKS = 2
 CHUNKS = 8
-EARLY = 6
+EARLY = 5
+WINDOW = 2
 AHEAD = 3
 MESH = pl.DeviceIdType.MESH
 F32 = jnp.float32
@@ -233,6 +234,12 @@
         r = crows(i)
         return remote(p1s.at[r], p1r.at[r], p1_ss.at[i], p1_rs.at[i], above, me)
 
+    def windowed(copy, i):
+        @pl.when(i >= WINDOW)
+        def _():
+            copy(i - WINDOW).wait_send()
+        copy(i).start()
+
     def relay_s1(i, _):
         @pl.when(jnp.logical_not(last))
         def _():
@@ -243,33 +250,20 @@
 
         @pl.when(jnp.logical_not(first))
         def _():
-            s1_copy(i).start()
+            windowed(s1_copy, i)
+
+        @pl.when(first)
+        def _():
+            p1s[r] = cbuf[1, r].astype(BF16)
+            windowed(p1_copy, i)
         gx_ref[1, r] = (go_ref[r].astype(F32) + s1).astype(BF16)
         return 0
 
-    def start_p1(i, _):
-        r = crows(i)
-        p1s[r] = cbuf[1, r].astype(BF16)
-        p1_copy(i).start()
-        return 0
-
     own_d1 = turn(1)
 
-    @pl.when(first)
-    def _():
-        lax.fori_loop(0, CHUNKS, start_p1, 0)
-
     lax.fori_loop(0, EARLY, relay_s1, 0)
-
-    @pl.when(last)
-    def _():
-        lax.fori_loop(EARLY, CHUNKS, relay_s1, 0)
-
     own_d0 = turn(0)
-
-    @pl.when(jnp.logical_not(last))
-    def _():
-        lax.fori_loop(EARLY, CHUNKS, relay_s1, 0)
+    lax.fori_loop(EARLY, CHUNKS, relay_s1, 0)
 
     def relay_s0(i, _):
         r = crows(i)
@@ -282,7 +276,7 @@
         @pl.when(jnp.logical_not(first))
         def _():
             s0s[r] = s0.astype(BF16)
-            s0_copy(i).start()
+            windowed(s0_copy, i)
         cbuf[0, r] = s0
         return 0
 
@@ -293,7 +287,7 @@
         def _():
             p1_copy(i).wait_recv()
             p1s[r] = (cbuf[1, r] + p1r[r].astype(F32)).astype(BF16)
-            p1_copy(i).start()
+            windowed(p1_copy, i)
         return 0
 
     def relay_both(i, _):
@@ -373,11 +367,11 @@
     def _():
         for b in range(BLOCKS):
             v_copy(0, b).wait_send()
-        lax.fori_loop(0, CHUNKS, sent_s, 0)
+        lax.fori_loop(CHUNKS - WINDOW, CHUNKS, sent_s, 0)
 
     @pl.when(jnp.logical_not(last))
     def _():
-        lax.fori_loop(0, CHUNKS, sent_p, 0)
+        lax.fori_loop(CHUNKS - WINDOW, CHUNKS, sent_p, 0)
 
 
 def on_device(saved, grad_out, gain, w_value):

time: 149 us -> 145 us (0.973)
  Pallas kernels: 143 us -> 138 us
    pallas_call x1, Pallas kernels: 143 us -> 138 us  [on_device(): pl.pallas_call(functools.partial(kernel, npipe, ndp), out_shape=(jax.Shap...]
where the time goes in v3:
time: 145 us
  Pallas kernels  138 us (95%)
  local copies, waits for them, and re-layouts  5.59 us (4%)
    pallas_call x1, Pallas kernels, on_device(): pl.pallas_call(functools.partial(kernel, npipe, ndp), out_shape=(jax.Shap...  138 us
    unnamed x5, local copies, waits for them, and re-layouts  5.59 us

profile of v3, /device:TPU:0, one launch (start us, length us, event | category | flops | bytes accessed | tf_op | source)
XLA Modules:
  0.0 144.7 jit_solution(7637261366897009386)
XLA Ops:
  0.6 1.4 copy.9
  2.0 138.5 %shard_map.59 = (bf16[2,128,4096]{2,1,0:T(8,128)(2,1)}, f32[512,512]{1,0:T(8,128)}) custom-call(bf16[2,128,4096]{2,1,0:T(8,128)(2,1)} %bitcast.9, bf16[128,4096]{1,0:T(8,128)(2,1)} %go_ref.1, f32[2,4096]{1,0:T(2,128)} %bitcast.13, bf16[512,512]{1,0:T(8,128)(2,1)} %bitcast.12), custom_call_target="tpu_custom_call" | custom-call | tf_op jit(solution)/shard_map/pallas_call | solution.py:385
  140.5 0.0 copy-start
  140.5 3.2 %copy.12 = bf16[2,1,128,4096]{3,2,1,0:T(8,128)(2,1)} copy(bf16[2,1,128,4096]{3,2,1,0:T(8,128)(2,1)} %bitcast.10) | data formatting | bytes 4194304
  143.7 0.0 copy-done
  143.7 1.0 copy.13
Async XLA Ops:
  140.5 3.2 %copy-start = (f32[512,512]{1,0:T(8,128)S(1)}, f32[512,512]{1,0:T(8,128)}, u32[]{:S(2)}) copy-start(f32[512,512]{1,0:T(8,128)} %get-tuple-element.5) | copy-start | bytes 3145732

commit v4 on v3

--- a/solution.py
+++ b/solution.py
@@ -128,7 +128,6 @@
         h_copy(j).start()
         return 0
 
-    lax.fori_loop(1, ndp, start_h, 0)
     own_h = pltpu.make_async_copy(hrows(me), hslot, loc.at[1])
     own_h.start()
 
@@ -260,6 +259,7 @@
         return 0
 
     own_d1 = turn(1)
+    lax.fori_loop(1, ndp, start_h, 0)
 
     lax.fori_loop(0, EARLY, relay_s1, 0)
     own_d0 = turn(0)

time: 145 us -> 145 us (level)
  no operation moved by 1% of the time
where the time goes in v4:
time: 145 us
  Pallas kernels  139 us (96%)
  local copies, waits for them, and re-layouts  5.59 us (4%)
    pallas_call x1, Pallas kernels, on_device(): pl.pallas_call(functools.partial(kernel, npipe, ndp), out_shape=(jax.Shap...  139 us
    unnamed x5, local copies, waits for them, and re-layouts  5.59 us

profile of v4, /device:TPU:0, one launch (start us, length us, event | category | flops | bytes accessed | tf_op | source)
XLA Modules:
  0.0 144.8 jit_solution(10050555342954056802)
XLA Ops:
  0.6 1.4 copy.9
  2.0 138.5 %shard_map.59 = (bf16[2,128,4096]{2,1,0:T(8,128)(2,1)}, f32[512,512]{1,0:T(8,128)}) custom-call(bf16[2,128,4096]{2,1,0:T(8,128)(2,1)} %bitcast.9, bf16[128,4096]{1,0:T(8,128)(2,1)} %go_ref.1, f32[2,4096]{1,0:T(2,128)} %bitcast.13, bf16[512,512]{1,0:T(8,128)(2,1)} %bitcast.12), custom_call_target="tpu_custom_call" | custom-call | tf_op jit(solution)/shard_map/pallas_call | solution.py:385
  140.6 0.0 copy-start
  140.6 3.2 %copy.12 = bf16[2,1,128,4096]{3,2,1,0:T(8,128)(2,1)} copy(bf16[2,1,128,4096]{3,2,1,0:T(8,128)(2,1)} %bitcast.10) | data formatting | bytes 4194304
  143.8 0.0 copy-done
  143.8 1.0 copy.13
Async XLA Ops:
  140.6 3.2 %copy-start = (f32[512,512]{1,0:T(8,128)S(1)}, f32[512,512]{1,0:T(8,128)}, u32[]{:S(2)}) copy-start(f32[512,512]{1,0:T(8,128)} %get-tuple-element.5) | copy-start | bytes 3145732

commit v5 on v4

--- a/solution.py
+++ b/solution.py
@@ -10,7 +10,7 @@
 HEAD = 128
 BLOCKS = 2
 CHUNKS = 8
-EARLY = 5
+EARLY = 2
 WINDOW = 2
 AHEAD = 3
 MESH = pl.DeviceIdType.MESH

time: 145 us -> 153 us (1.055)
  Pallas kernels: 139 us -> 146 us
    pallas_call x1, Pallas kernels: 139 us -> 146 us  [on_device(): pl.pallas_call(functools.partial(kernel, npipe, ndp), out_shape=(jax.Shap...]
where the time goes in v5:
time: 153 us; the launch traced here: 152 us
  Pallas kernels  146 us (95%)
  local copies, waits for them, and re-layouts  5.59 us (4%)
    pallas_call x1, Pallas kernels, on_device(): pl.pallas_call(functools.partial(kernel, npipe, ndp), out_shape=(jax.Shap...  146 us
    unnamed x5, local copies, waits for them, and re-layouts  5.59 us

profile of v5, /device:TPU:0, one launch (start us, length us, event | category | flops | bytes accessed | tf_op | source)
XLA Modules:
  0.0 152.5 jit_solution(537773818705268001)
XLA Ops:
  0.6 1.4 copy.9
  2.0 146.3 %shard_map.59 = (bf16[2,128,4096]{2,1,0:T(8,128)(2,1)}, f32[512,512]{1,0:T(8,128)}) custom-call(bf16[2,128,4096]{2,1,0:T(8,128)(2,1)} %bitcast.9, bf16[128,4096]{1,0:T(8,128)(2,1)} %go_ref.1, f32[2,4096]{1,0:T(2,128)} %bitcast.13, bf16[512,512]{1,0:T(8,128)(2,1)} %bitcast.12), custom_call_target="tpu_custom_call" | custom-call | tf_op jit(solution)/shard_map/pallas_call | solution.py:385
  148.3 0.0 copy-start
  148.3 3.2 %copy.12 = bf16[2,1,128,4096]{3,2,1,0:T(8,128)(2,1)} copy(bf16[2,1,128,4096]{3,2,1,0:T(8,128)(2,1)} %bitcast.10) | data formatting | bytes 4194304
  151.5 0.0 copy-done
  151.5 1.0 copy.13
Async XLA Ops:
  148.3 3.2 %copy-start = (f32[512,512]{1,0:T(8,128)S(1)}, f32[512,512]{1,0:T(8,128)}, u32[]{:S(2)}) copy-start(f32[512,512]{1,0:T(8,128)} %get-tuple-element.5) | copy-start | bytes 3145732
